TPU v7x, 32 devices: a whole 2x2x4 slice. The times are simulated.
32 devices in a mesh: band: 4 (over y, core), ga: 8 (over z, x).
Axes of the slice: x: 2, y: 2, z: 4, core: 2. Of those that a mesh axis runs over, the one named last changes fastest.
Arguments:
- density: float32 [160, 160, 160], P('ga'), may hold values from -6 to 6
- stick_column: int32 [20480], replicated, may hold values from 0 to 25599, as said below
- vloc: float32 [2, 160, 20480], P(None, None, 'ga'), may hold values from -0.0034179688 to 0.0034179688
- positions: float32 [3, 32], replicated, may hold values from 0 to 1
- species: int32 [32], replicated, may hold values from 0 to 1
- psi: bfloat16 [270336, 2, 1024], P('ga', None, 'band'), may hold values from -6 to 6
- miller_wave: int32 [3, 270336], P(None, 'ga'), may hold values from -40 to 40
- proj_radial: float32 [2, 8, 270336], P(None, None, 'ga'), may hold values from -0.01171875 to 0.01171875
- proj_count: int32 [2], replicated, may hold values from 4 to 8
- dcoef: float32 [2, 8, 8], replicated, may hold values from -0.0625 to 0.0625
- occupation: float32 [1024], P('band'), may hold values from 0 to 2
Outputs:
- density_sticks: float32 [2, 160, 20480], P(None, None, 'ga')
- forces: float32 [3, 32], replicated
Inputs may be any that keep to these rules, and one draw needn't show every extreme that they name: `stick_column`: distinct columns of the 160 by 160 frequency plane.
All inputs are finite; a program needn't handle non-finite values.
Results may differ from a plain program's by a relative error of at most 0.0036.
Values sent between devices are 32-bit elements; how exact they have to be, the bound alone decides.
A program may use at most 192 MiB of HBM per device.

v0:
```python
import math

import jax
import jax.numpy as jnp
from jax import lax
from jax.sharding import PartitionSpec as P

NX = 160
NY = 160
NZ = 160


TWO_PI = 2.0 * math.pi
EXACT = lax.Precision.HIGHEST


def frequency(index, count):
    return jnp.where(index >= count // 2, index - count, index)


def dft_table(count):
    index = jnp.arange(count, dtype=jnp.int32)
    angle = TWO_PI / count * (index[:, None] * index[None, :] % count).astype(jnp.float32)
    return (jnp.cos(angle), jnp.sin(angle))


def shards(
    density,
    stick_column,
    vloc,
    positions,
    species,
    psi,
    miller_wave,
    proj_radial,
    proj_count,
    dcoef,
    occupation,
):
    ga_index = lax.axis_index("ga")
    band_index = lax.axis_index("band")
    ga_count = lax.axis_size("ga")
    band_count = lax.axis_size("band")
    atom_count = positions.shape[1]
    kind_count = vloc.shape[0]
    slot_count = proj_radial.shape[1]
    sticks_here = vloc.shape[2]
    planes = density.shape[0]
    scale_norm = 1.0 / math.sqrt(NX * NY * NZ)
    start_zero = jnp.int32(0)
    cos_y, sin_y = dft_table(NY)
    cos_x, sin_x = dft_table(NX)
    batch_cos = jnp.broadcast_to(cos_x[None], (planes, NX, NX))
    batch_sin = jnp.broadcast_to(sin_x[None], (planes, NX, NX))
    xpass_real = jnp.einsum("pmx,pxy->pmy", batch_cos, density, precision=EXACT).reshape(
        planes * NX, NY
    )
    xpass_imag = -jnp.einsum("pmx,pxy->pmy", batch_sin, density, precision=EXACT).reshape(
        planes * NX, NY
    )
    full_real = jnp.dot(xpass_real, cos_y, precision=EXACT) + jnp.dot(
        xpass_imag, sin_y, precision=EXACT
    )
    full_imag = jnp.dot(xpass_imag, cos_y, precision=EXACT) - jnp.dot(
        xpass_real, sin_y, precision=EXACT
    )
    columns = jnp.concatenate(
        [full_real.reshape(planes, NX * NY), full_imag.reshape(planes, NX * NY)], axis=0
    )
    picked_rows = jnp.take(columns.T, stick_column, axis=0)
    chosen = picked_rows.T.reshape(2, planes, stick_column.shape[0])
    by_stick = lax.all_to_all(chosen, "ga", split_axis=2, concat_axis=1, tiled=True)
    cos_z, sin_z = dft_table(NZ)
    stick_real = (
        jnp.dot(cos_z, by_stick[0], precision=EXACT) + jnp.dot(sin_z, by_stick[1], precision=EXACT)
    ) * scale_norm
    stick_imag = (
        jnp.dot(cos_z, by_stick[1], precision=EXACT) - jnp.dot(sin_z, by_stick[0], precision=EXACT)
    ) * scale_norm
    density_sticks = jnp.stack([stick_real, stick_imag])
    owned = lax.dynamic_slice_in_dim(stick_column, ga_index * sticks_here, sticks_here)
    freq_x = frequency(owned // NY, NX).astype(jnp.float32)
    freq_y = frequency(owned % NY, NY).astype(jnp.float32)
    freq_z = frequency(jnp.arange(NZ, dtype=jnp.int32), NZ).astype(jnp.float32)
    wave_x = TWO_PI / NX * freq_x
    wave_y = TWO_PI / NY * freq_y
    wave_z = TWO_PI / NZ * freq_z
    per_band = atom_count // band_count
    band_start = band_index * per_band
    band_places = lax.dynamic_slice_in_dim(positions, band_start, per_band, 1)
    band_kinds = lax.dynamic_slice_in_dim(species, band_start, per_band)
    angle_plane = TWO_PI * (
        band_places[0][:, None] * freq_x[None, :] + band_places[1][:, None] * freq_y[None, :]
    )
    angle_depth = TWO_PI * band_places[2][:, None] * freq_z[None, :]
    channel_real = []
    channel_imag = []
    for kind_index in range(kind_count):
        base_real = vloc[kind_index] * stick_real
        base_imag = vloc[kind_index] * stick_imag
        for source, target in ((base_real, channel_real), (base_imag, channel_imag)):
            target.append(source * wave_x[None, :])
            target.append(source * wave_y[None, :])
            target.append(source * wave_z[:, None])
    field_real = jnp.stack(channel_real)
    field_imag = jnp.stack(channel_imag)
    plane_cos = jnp.cos(angle_plane)
    plane_sin = jnp.sin(angle_plane)
    summed_real = jnp.einsum("ak,qzk->aqz", plane_cos, field_real, precision=EXACT) - jnp.einsum(
        "ak,qzk->aqz", plane_sin, field_imag, precision=EXACT
    )
    summed_imag = jnp.einsum("ak,qzk->aqz", plane_cos, field_imag, precision=EXACT) + jnp.einsum(
        "ak,qzk->aqz", plane_sin, field_real, precision=EXACT
    )
    along_depth = jnp.sum(
        jnp.cos(angle_depth)[:, None, :] * summed_imag
        + jnp.sin(angle_depth)[:, None, :] * summed_real,
        axis=2,
    )
    along_depth = along_depth.reshape(per_band, kind_count, 3)
    band_pick = (band_kinds[:, None] == jnp.arange(kind_count, dtype=jnp.int32)[None, :]).astype(
        jnp.float32
    )
    local_part = jnp.einsum("asc,as->ca", along_depth, band_pick, precision=EXACT)
    local_full = lax.dynamic_update_slice(
        jnp.zeros((3, atom_count), jnp.float32), local_part, (start_zero, band_start)
    )
    local_total = lax.psum(local_full, ("band", "ga"))
    bands_here = psi.shape[2]
    waves_here = psi.shape[0]
    psi_flat = psi.reshape(waves_here, 2 * bands_here)
    miller_f = miller_wave.astype(jnp.float32)
    weights = jnp.stack(
        [
            jnp.ones_like(miller_f[0]),
            TWO_PI / NX * miller_f[0],
            TWO_PI / NY * miller_f[1],
            TWO_PI / NZ * miller_f[2],
        ]
    )

    def project_block(block_start, block_rows):
        block_atoms = block_rows // slot_count
        atom_start = block_start // slot_count
        block_places = lax.dynamic_slice_in_dim(positions, atom_start, block_atoms, 1)
        block_kinds = lax.dynamic_slice_in_dim(species, atom_start, block_atoms)
        phase = TWO_PI * (
            block_places[0][:, None] * miller_f[0][None, :]
            + block_places[1][:, None] * miller_f[1][None, :]
            + block_places[2][:, None] * miller_f[2][None, :]
        )
        radial = jnp.zeros((block_atoms, slot_count, waves_here), jnp.float32)
        for kind_index in range(kind_count):
            match = (block_kinds == kind_index).astype(jnp.float32)
            radial = radial + match[:, None, None] * proj_radial[kind_index][None]
        parts = jnp.stack(
            [radial * jnp.cos(phase)[:, None, :], radial * jnp.sin(phase)[:, None, :]], axis=2
        )
        table = (parts[:, :, None] * weights[None, None, :, None, :]).astype(jnp.bfloat16)
        product = jnp.dot(
            table.reshape(block_rows * 8, waves_here), psi_flat, preferred_element_type=jnp.float32
        )
        product = product.reshape(block_rows, 4, 2, 2, bands_here)
        proj_real = product[:, :, 0, 0] - product[:, :, 1, 1]
        proj_imag = product[:, :, 0, 1] + product[:, :, 1, 0]
        return jnp.stack([proj_real, proj_imag], axis=2).reshape(block_rows, 8 * bands_here)

    share_rows = atom_count * slot_count // ga_count
    block_rows = 64
    starts = block_rows * jnp.arange(
        share_rows * lax.axis_size("ga") // block_rows, dtype=jnp.int32
    )

    def one_block(block_start):
        return project_block(block_start, block_rows)

    owned_rows = lax.psum_scatter(
        lax.map(one_block, starts).reshape(share_rows * lax.axis_size("ga"), 8 * bands_here),
        "ga",
        scatter_dimension=0,
        tiled=True,
    )
    per_ga = share_rows // slot_count
    ga_start = ga_index * per_ga
    terms = owned_rows.reshape(per_ga, slot_count, 4, 2, bands_here)
    ga_kinds = lax.dynamic_slice_in_dim(species, ga_start, per_ga)
    ga_pick = (ga_kinds[:, None] == jnp.arange(kind_count, dtype=jnp.int32)[None, :]).astype(
        jnp.float32
    )
    live_slots = (jnp.arange(slot_count, dtype=jnp.int32)[None, :] < proj_count[:, None]).astype(
        jnp.float32
    )
    kind_table = dcoef * live_slots[:, :, None] * live_slots[:, None, :]
    coupling = jnp.einsum("as,sij->aij", ga_pick, kind_table, precision=EXACT)
    mixed_real = jnp.einsum("aij,ajcn->aicn", coupling, terms[:, :, 1:, 0], precision=EXACT)
    mixed_imag = jnp.einsum("aij,ajcn->aicn", coupling, terms[:, :, 1:, 1], precision=EXACT)
    value = (
        terms[:, :, 0, 0][:, :, None, :] * mixed_imag
        - terms[:, :, 0, 1][:, :, None, :] * mixed_real
    )
    nonlocal_part = 2.0 * jnp.einsum("aicn,n->ca", value, occupation, precision=EXACT)
    nonlocal_full = lax.dynamic_update_slice(
        jnp.zeros((3, atom_count), jnp.float32), nonlocal_part, (start_zero, ga_start)
    )
    forces = local_total + lax.psum(nonlocal_full, ("band", "ga"))
    return (density_sticks, forces)


def solution(mesh):
    in_specs = (
        P("ga", None, None),
        P(),
        P(None, None, "ga"),
        P(),
        P(),
        P("ga", None, "band"),
        P(None, "ga"),
        P(None, None, "ga"),
        P(),
        P(),
        P("band"),
    )
    out_specs = (P(None, None, "ga"), P())
    return jax.shard_map(shards, mesh=mesh, in_specs=in_specs, out_specs=out_specs, check_vma=False)
```

profile of v0, /device:TPU:0, one launch (start us, length us, event | category | flops | bytes accessed | tf_op | source)
XLA Modules:
  0.0 747.2 jit_solution(12256284340783067655)
XLA Ops:
  20.4 5.5 fusion.45
  25.9 4.0 convolution_add_fusion
  32.3 5.6 reshape.541
  37.9 6.8 convolution_subtract_fusion
  47.3 4.0 reshape.542
  51.3 4.7 pad_maximum_fusion.2
  56.0 9.0 %copy.65 = f32[40,25600]{0,1:T(8,128)} copy(f32[40,25600]{1,0:T(8,128)} %pad_maximum_fusion.2) | data formatting | bytes 8192000 | tf_op jit(solution)/shard_map/concatenate | solution.py:67
  65.0 73.2 %gather_fusion = f32[20480,40]{1,0:T(8,128)} fusion(f32[25600,40]{1,0:T(8,128)} %bitcast.221, s32[20480]{0:T(1024)S(1)} %fusion.53), kind=kCustom, calls=%fused_computation | custom fusion | bytes 6635520 | tf_op jit(solution)/shard_map/jit(_take)/gather | solution.py:70
  138.2 12.8 %select_bitcast_fusion = f32[40,20480]{0,1:T(8,128)} fusion(f32[20480,40]{1,0:T(8,128)} %gather_fusion, pred[20480]{0:T(1024)(128)(4,1)S(1)} %compare_and_fusion), kind=kLoop, calls=%fused_computation.31 | loop fusion | flops 819200 | bytes 6574080 | tf_op jit(solution)/shard_map/jit(_take)/select_n | solution.py:70
  150.9 20.9 %reshape.568 = f32[2,20,20480]{1,0,2:T(2,128)} reshape(f32[40,20480]{0,1:T(8,128)} %select_bitcast_fusion) | data formatting | bytes 6553600 | tf_op jit(solution)/shard_map/reshape | solution.py:71
  171.9 49.0 %reshape.570 = f32[8,1,102400]{2,1,0:T(1,128)} reshape(f32[20480,2,20]{2,1,0:T(2,128)} %bitcast.223) | data formatting | bytes 6553600
  220.9 7.4 all-to-all-start
  231.2 83.8 %copy.71 = bf16[33792,2,256]{0,2,1:T(8,128)(2,1)} copy(bf16[33792,2,256]{2,1,0:T(2,128)(2,1)} %param.18) | data formatting | bytes 69206016 | tf_op args[5]
  316.4 181.3 %while.12 = (s32[]{:T(128)}, f32[4,64,2048]{2,1,0:T(8,128)}, s32[4]{0:T(128)S(1)}, s32[32]{0:T(128)S(1)}, f32[2,8,33792]{2,1,0:T(8,128)}, /*index=5*/f32[3,32]{1...) while((s32[]{:T(128)}, f32[4,64,2048]{2,1,0:T(8,128)}, ...), condition=%wide.region_3.4_spmd, body=%wide.region_2.3_spmd.sunk | while | flops 17768366080 | bytes 125361648 | solution.py:178
  329.4 6.2 pad_maximum_fusion.7
  335.6 24.2 %fusion.149 = f32[64,4,2,2,256]{4,0,3,2,1:T(8,128)S(1)} fusion(bf16[2,256,33792,1,1]{2,1,0,4,3:T(8,128)(2,1)} %bitcast.227, f32[4,33792]{1,0:T(4,128)S(1)} %copy-done.11, f32[64,2,33792]{2,0,1:T(8,128)} %pad_maximum_fusion.7), kind=kOutput, calls=%fused_computation.3.clone.1 | convolution fusion | flops 17751343104 | bytes 53493760 | tf_op jit(solution)/shard_map/while/body/eval_jaxpr/dot_general | solution.py:160
  374.6 6.2 pad_maximum_fusion.7
  380.8 24.2 %fusion.149 = f32[64,4,2,2,256]{4,0,3,2,1:T(8,128)S(1)} fusion(bf16[2,256,33792,1,1]{2,1,0,4,3:T(8,128)(2,1)} %bitcast.227, f32[4,33792]{1,0:T(4,128)S(1)} %copy-done.11, f32[64,2,33792]{2,0,1:T(8,128)} %pad_maximum_fusion.7), kind=kOutput, calls=%fused_computation.3.clone.1 | convolution fusion | flops 17751343104 | bytes 53493760 | tf_op jit(solution)/shard_map/while/body/eval_jaxpr/dot_general | solution.py:160
  419.8 6.2 pad_maximum_fusion.7
  426.0 24.2 %fusion.149 = f32[64,4,2,2,256]{4,0,3,2,1:T(8,128)S(1)} fusion(bf16[2,256,33792,1,1]{2,1,0,4,3:T(8,128)(2,1)} %bitcast.227, f32[4,33792]{1,0:T(4,128)S(1)} %copy-done.11, f32[64,2,33792]{2,0,1:T(8,128)} %pad_maximum_fusion.7), kind=kOutput, calls=%fused_computation.3.clone.1 | convolution fusion | flops 17751343104 | bytes 53493760 | tf_op jit(solution)/shard_map/while/body/eval_jaxpr/dot_general | solution.py:160
  465.1 6.2 pad_maximum_fusion.7
  471.2 24.2 %fusion.149 = f32[64,4,2,2,256]{4,0,3,2,1:T(8,128)S(1)} fusion(bf16[2,256,33792,1,1]{2,1,0,4,3:T(8,128)(2,1)} %bitcast.227, f32[4,33792]{1,0:T(4,128)S(1)} %copy-done.11, f32[64,2,33792]{2,0,1:T(8,128)} %pad_maximum_fusion.7), kind=kOutput, calls=%fused_computation.3.clone.1 | convolution fusion | flops 17751343104 | bytes 53493760 | tf_op jit(solution)/shard_map/while/body/eval_jaxpr/dot_general | solution.py:160
  499.4 68.2 %reduce-scatter.2.cloned.1.call-done = f32[32,2048]{1,0:T(8,128)} async-done(((f32[256,2048]{1,0:T(8,128)}), f32[32,2048]{1,0:T(8,128)}) %reduce-scatter.2.cloned.1.call-update) | async-done | bytes 262160 | tf_op jit(solution)/shard_map/reduce_scatter | solution.py:177
  570.5 10.4 %reduce.2 = f32[8,102400]{1,0:T(8,128)S(1)} reduce(f32[8,1,102400]{2,1,0:T(1,128)} %all-to-all-done, f32[]{:T(128)} %broadcast.500), dimensions={1}, to_apply=%all_to_all.11.reduce_sub_computation | reduce | bytes 6553604 | tf_op jit(solution)/shard_map/all_to_all | solution.py:72
  580.9 42.1 %reshape.571 = f32[20480,2,20]{2,1,0:T(2,128)} reshape(f32[8,102400]{1,0:T(8,128)S(1)} %reduce.2) | data formatting | bytes 6553600
  623.0 16.8 %copy.87 = f32[2,20,8,2560]{3,2,0,1:T(8,128)S(1)} copy(f32[2,20,8,2560]{1,0,3,2:T(2,128)} %bitcast.224) | data formatting | bytes 6553600 | tf_op jit(solution)/shard_map/all_to_all | solution.py:72
  662.2 8.4 %fusion.31 = f32[8,6,160]{2,0,1:T(8,128)S(1)} fusion(f32[6,160,2560]{2,1,0:T(8,128)S(1)} %get-tuple-element.161, f32[2560]{0:T(1024)S(1)} %get-tuple-element.136, f32[8]{0:T(128)S(1)} %get-tuple-element.177, f32[2560]{0:T(1024)S(1)} %get-tuple-element.175, f32[8]{0:T(128)S(1)} %get-tuple-element.178), kind=kOutput, calls=%fused_computation.89 | convolution fusion | flops 236011520 | bytes 9881664 | tf_op jit(solution)/shard_map/ak,qzk->aqz/dot_general | solution.py:109
  670.6 8.3 %fusion.33 = f32[8,6,160]{2,0,1:T(8,128)S(1)} fusion(f32[6,160,2560]{2,1,0:T(8,128)S(1)} %get-tuple-element.162, f32[2560]{0:T(1024)S(1)} %get-tuple-element.136, f32[8]{0:T(128)S(1)} %get-tuple-element.177, f32[2560]{0:T(1024)S(1)} %get-tuple-element.175, f32[8]{0:T(128)S(1)} %get-tuple-element.178), kind=kOutput, calls=%fused_computation.91 | convolution fusion | flops 236011520 | bytes 9881664 | tf_op jit(solution)/shard_map/ak,qzk->aqz/dot_general | solution.py:112
  678.9 8.5 %fusion.20 = f32[8,6,160]{2,0,1:T(8,128)S(1)} fusion(f32[8,6,160]{2,0,1:T(8,128)S(1)} %fusion.33, f32[6,160,2560]{2,1,0:T(8,128)S(1)} %get-tuple-element.161, f32[2560]{0:T(1024)S(1)} %get-tuple-element.136, f32[8]{0:T(128)S(1)} %get-tuple-element.177, f32[2560]{0:T(1024)S(1)} %get-tuple-element.175, f32[8]{0:T(128)S(1)} %get-tuple-element.178, ...), kind=kOutput, calls=%fused_computation.68 | convolution fusion | flops 236026880 | bytes 9917504 | tf_op jit(solution)/shard_map/ak,qzk->aqz/dot_general | solution.py:112
  687.5 8.4 %fusion.21 = f32[8,6]{0,1:T(8,128)S(1)} fusion(f32[8,6,160]{2,0,1:T(8,128)S(1)} %fusion.20, f32[8,6,160]{2,0,1:T(8,128)S(1)} %fusion.31, f32[6,160,2560]{2,1,0:T(8,128)S(1)} %get-tuple-element.162, f32[2560]{0:T(1024)S(1)} %get-tuple-element.136, f32[8]{0:T(128)S(1)} %get-tuple-element.177, f32[2560]{0:T(1024)S(1)} %get-tuple-element.175, ...), kind=kOutput, calls=%fused_computation.69 | convolution fusion | flops 236042192 | bytes 9917696 | tf_op jit(solution)/shard_map/ak,qzk->aqz/dot_general | solution.py:109
  696.2 39.7 %psum.16 = f32[3,32]{1,0:T(4,128)} all-reduce(f32[3,32]{1,0:T(4,128)S(1)} %dynamic-update-slice), channel_id=1, replica_groups=mesh['band'=4,'ga'=8] {'band','ga'}, use_global_device_ids=true, to_apply=%region_1.2 | all-reduce | flops 96 | bytes 768 | tf_op jit(solution)/shard_map/psum | solution.py:128
  735.9 4.0 pad_maximum_fusion.3
  (174 shorter events, 99.4 us)
Async XLA Ops:
  7.2 3.1 copy-start
  13.4 7.0 copy-start.4
  32.3 5.6 copy-start.5
  220.9 7.5 %copy-start.12 = (s32[3,33792]{1,0:T(4,128)S(1)}, s32[3,33792]{1,0:T(4,128)}, u32[]{:S(2)}) copy-start(s32[3,33792]{1,0:T(4,128)} %param.19) | copy-start | bytes 1216516
  220.9 349.1 %all-to-all-start = ((f32[8,1,102400]{2,1,0:T(1,128)}), f32[8,1,102400]{2,1,0:T(1,128)}, u32[]{:S(2)}, u32[]{:S(2)}) async-start(f32[8,1,102400]{2,1,0:T(1,128)} %reshape.570), calls=%async_computation | async-start | bytes 6553600 | tf_op jit(solution)/shard_map/all_to_all | solution.py:72
  228.3 339.3 %reduce-scatter.2.cloned.1.call-start = ((), (), s32[]{:S(2)}) async-start(), calls=%async_computation.2 | async-start | bytes 2359296 | tf_op jit(solution)/shard_map/reduce_scatter | solution.py:177
  231.2 85.2 %copy-start.13 = (f32[3,32]{1,0:T(4,128)S(1)}, f32[3,32]{1,0:T(4,128)}, u32[]{:S(2)}) copy-start(f32[3,32]{1,0:T(4,128)} %param.16) | copy-start | bytes 1156
  231.2 85.1 %copy-start.14 = (s32[32]{0:T(128)S(1)}, s32[32]{0:T(128)}, u32[]{:S(2)}) copy-start(s32[32]{0:T(128)} %param.17) | copy-start | bytes 388
  316.4 181.7 %copy-start.17 = (s32[2]{0:T(128)S(1)}, s32[2]{0:T(128)}, u32[]{:S(2)}) copy-start(s32[2]{0:T(128)} %param.21) | copy-start | bytes 28
  316.4 181.8 %copy-start.15 = (f32[2,8,8]{2,1,0:T(8,128)S(1)}, f32[2,8,8]{2,1,0:T(8,128)}, u32[]{:S(2)}) copy-start(f32[2,8,8]{2,1,0:T(8,128)} %param.22) | copy-start | bytes 1540
  329.4 6.2 copy-start.11
  374.6 6.2 copy-start.11
  419.8 6.2 copy-start.11
  465.0 6.2 copy-start.11
  497.7 71.9 %copy-start.16 = (f32[256]{0:T(256)S(1)}, f32[256]{0:T(256)}, u32[]{:S(2)}) copy-start(f32[256]{0:T(256)} %param.23) | copy-start | bytes 3076
  643.4 5.1 copy-start.9
  645.1 5.6 copy-start.7
  652.7 2.2 copy-start.10
  654.9 2.3 copy-start.6
  654.9 2.4 copy-start.8
  657.2 4.5 copy-start.2
  659.8 1.9 copy-start.3
  735.9 4.0 copy-start.1
Sparse Core Ops, SparseCore 0:
  497.8 69.7 reduce-scatter.1
where the time goes:
time: 760 us; the launch traced here: 747 us
  local copies, waits for them, and re-layouts  346 us (46%)
  matrix products  168 us (22%)
  other arithmetic  92.7 us (12%)
  waiting for transfers between devices  68.2 us (9%)
  blocking collectives  39.7 us (5%)
  between operations  14.9 us (2%)
  loops' own time  9.85 us (1%)
    unnamed x39, local copies, waits for them, and re-layouts  175 us
    dot_general x4, matrix products, project_block(): jnp.dot(table.reshape(block_rows * 8, waves_here), psi_flat, preferred_el...  96.8 us
    gather x1, local copies, waits for them, and re-layouts, shards(): picked_rows = jnp.take(columns.T, stick_column, axis=0)  73.2 us
    reduce_scatter x1, waiting for transfers between devices, shards(): lax.psum_scatter(lax.map(one_block, starts).reshape(share_rows * lax.axis...  68.2 us
    psum x1, blocking collectives, shards(): local_total = lax.psum(local_full, ('band', 'ga'))  39.7 us
    another operation x4, other arithmetic, project_block(): jnp.stack([radial * jnp.cos(phase)[:, None, :], radial * jnp.sin(phase)[:...  24.7 us
    reshape x1, local copies, waits for them, and re-layouts, shards(): chosen = picked_rows.T.reshape(2, planes, stick_column.shape[0])  20.9 us
    all_to_all x2, local copies, waits for them, and re-layouts, shards(): lax.all_to_all(chosen, 'ga', split_axis=2, concat_axis=1, tiled=True)  17.3 us
  transfers between devices with their start and end apart: 2, of which 1 were waited for; matrix products, arithmetic and copies ran while one was open for 35% of the time, Pallas kernels for 0%

commit v1 on v0

--- a/solution.py
+++ b/solution.py
@@ -12,6 +12,7 @@
 
 TWO_PI = 2.0 * math.pi
 EXACT = lax.Precision.HIGHEST
+FINE = lax.Precision.HIGH
 
 
 def frequency(index, count):
@@ -52,80 +53,79 @@
     cos_x, sin_x = dft_table(NX)
     batch_cos = jnp.broadcast_to(cos_x[None], (planes, NX, NX))
     batch_sin = jnp.broadcast_to(sin_x[None], (planes, NX, NX))
-    xpass_real = jnp.einsum("pmx,pxy->pmy", batch_cos, density, precision=EXACT).reshape(
+    xpass_real = jnp.einsum("pmx,pxy->pmy", batch_cos, density, precision=FINE).reshape(
         planes * NX, NY
     )
-    xpass_imag = -jnp.einsum("pmx,pxy->pmy", batch_sin, density, precision=EXACT).reshape(
+    xpass_imag = -jnp.einsum("pmx,pxy->pmy", batch_sin, density, precision=FINE).reshape(
         planes * NX, NY
     )
-    full_real = jnp.dot(xpass_real, cos_y, precision=EXACT) + jnp.dot(
-        xpass_imag, sin_y, precision=EXACT
-    )
-    full_imag = jnp.dot(xpass_imag, cos_y, precision=EXACT) - jnp.dot(
-        xpass_real, sin_y, precision=EXACT
+    full_real = jnp.dot(xpass_real, cos_y, precision=FINE) + jnp.dot(
+        xpass_imag, sin_y, precision=FINE
+    )
+    full_imag = jnp.dot(xpass_imag, cos_y, precision=FINE) - jnp.dot(
+        xpass_real, sin_y, precision=FINE
     )
     columns = jnp.concatenate(
         [full_real.reshape(planes, NX * NY), full_imag.reshape(planes, NX * NY)], axis=0
     )
-    picked_rows = jnp.take(columns.T, stick_column, axis=0)
-    chosen = picked_rows.T.reshape(2, planes, stick_column.shape[0])
-    by_stick = lax.all_to_all(chosen, "ga", split_axis=2, concat_axis=1, tiled=True)
+    sub_sticks = sticks_here // band_count
+    share_columns = lax.dynamic_slice_in_dim(
+        stick_column.reshape(ga_count, band_count, sub_sticks), band_index, 1, 1
+    ).reshape(ga_count * sub_sticks)
+    picked_rows = jnp.take(columns.T, share_columns, axis=0)
+    chosen = picked_rows.T.reshape(2 * planes, ga_count, sub_sticks).transpose(1, 0, 2)
+    by_stick = lax.all_to_all(chosen, "ga", split_axis=0, concat_axis=0, tiled=True)
+    by_stick = by_stick.reshape(ga_count * 2 * planes, sub_sticks)
     cos_z, sin_z = dft_table(NZ)
-    stick_real = (
-        jnp.dot(cos_z, by_stick[0], precision=EXACT) + jnp.dot(sin_z, by_stick[1], precision=EXACT)
-    ) * scale_norm
-    stick_imag = (
-        jnp.dot(cos_z, by_stick[1], precision=EXACT) - jnp.dot(sin_z, by_stick[0], precision=EXACT)
-    ) * scale_norm
-    density_sticks = jnp.stack([stick_real, stick_imag])
-    owned = lax.dynamic_slice_in_dim(stick_column, ga_index * sticks_here, sticks_here)
+    cos_z = cos_z.reshape(NZ, ga_count, planes) * scale_norm
+    sin_z = sin_z.reshape(NZ, ga_count, planes) * scale_norm
+    table_z = jnp.stack(
+        [jnp.stack([cos_z, sin_z], axis=2), jnp.stack([-sin_z, cos_z], axis=2)]
+    ).reshape(2 * NZ, ga_count * 2 * planes)
+    sub_values = jnp.dot(table_z, by_stick, precision=FINE).reshape(2, NZ, sub_sticks)
+    density_sticks = lax.all_gather(sub_values, "band", axis=2, tiled=True)
+    stick_start = ga_index * sticks_here + band_index * sub_sticks
+    owned = lax.dynamic_slice_in_dim(stick_column, stick_start, sub_sticks)
     freq_x = frequency(owned // NY, NX).astype(jnp.float32)
     freq_y = frequency(owned % NY, NY).astype(jnp.float32)
     freq_z = frequency(jnp.arange(NZ, dtype=jnp.int32), NZ).astype(jnp.float32)
     wave_x = TWO_PI / NX * freq_x
     wave_y = TWO_PI / NY * freq_y
     wave_z = TWO_PI / NZ * freq_z
-    per_band = atom_count // band_count
-    band_start = band_index * per_band
-    band_places = lax.dynamic_slice_in_dim(positions, band_start, per_band, 1)
-    band_kinds = lax.dynamic_slice_in_dim(species, band_start, per_band)
     angle_plane = TWO_PI * (
-        band_places[0][:, None] * freq_x[None, :] + band_places[1][:, None] * freq_y[None, :]
-    )
-    angle_depth = TWO_PI * band_places[2][:, None] * freq_z[None, :]
-    channel_real = []
-    channel_imag = []
-    for kind_index in range(kind_count):
-        base_real = vloc[kind_index] * stick_real
-        base_imag = vloc[kind_index] * stick_imag
-        for source, target in ((base_real, channel_real), (base_imag, channel_imag)):
-            target.append(source * wave_x[None, :])
-            target.append(source * wave_y[None, :])
-            target.append(source * wave_z[:, None])
-    field_real = jnp.stack(channel_real)
-    field_imag = jnp.stack(channel_imag)
+        positions[0][:, None] * freq_x[None, :] + positions[1][:, None] * freq_y[None, :]
+    )
+    angle_depth = TWO_PI * positions[2][:, None] * freq_z[None, :]
     plane_cos = jnp.cos(angle_plane)
     plane_sin = jnp.sin(angle_plane)
-    summed_real = jnp.einsum("ak,qzk->aqz", plane_cos, field_real, precision=EXACT) - jnp.einsum(
-        "ak,qzk->aqz", plane_sin, field_imag, precision=EXACT
-    )
-    summed_imag = jnp.einsum("ak,qzk->aqz", plane_cos, field_imag, precision=EXACT) + jnp.einsum(
-        "ak,qzk->aqz", plane_sin, field_real, precision=EXACT
-    )
-    along_depth = jnp.sum(
-        jnp.cos(angle_depth)[:, None, :] * summed_imag
-        + jnp.sin(angle_depth)[:, None, :] * summed_real,
+    plane_rows = jnp.stack(
+        [
+            plane_cos * wave_x[None, :],
+            plane_cos * wave_y[None, :],
+            plane_cos,
+            plane_sin * wave_x[None, :],
+            plane_sin * wave_y[None, :],
+            plane_sin,
+        ]
+    ).reshape(6 * atom_count, sub_sticks)
+    vloc_here = lax.dynamic_slice_in_dim(vloc, band_index * sub_sticks, sub_sticks, 2)
+    fields = (vloc_here[:, None] * sub_values[None]).reshape(kind_count * 2 * NZ, sub_sticks)
+    sums = lax.dot_general(plane_rows, fields, (((1,), (1,)), ((), ())), precision=FINE)
+    sums = sums.reshape(2, 3, atom_count, kind_count, 2, NZ)
+    all_pick = (species[:, None] == jnp.arange(kind_count, dtype=jnp.int32)[None, :]).astype(
+        jnp.float32
+    )
+    sums = jnp.sum(sums * all_pick[None, None, :, :, None, None], axis=3)
+    summed_real = sums[0, :, :, 0] - sums[1, :, :, 1]
+    summed_imag = sums[0, :, :, 1] + sums[1, :, :, 0]
+    depth_weight = jnp.stack([jnp.ones_like(wave_z), jnp.ones_like(wave_z), wave_z])
+    local_part = jnp.sum(
+        (
+            jnp.cos(angle_depth)[None] * summed_imag + jnp.sin(angle_depth)[None] * summed_real
+        )
+        * depth_weight[:, None, :],
         axis=2,
     )
-    along_depth = along_depth.reshape(per_band, kind_count, 3)
-    band_pick = (band_kinds[:, None] == jnp.arange(kind_count, dtype=jnp.int32)[None, :]).astype(
-        jnp.float32
-    )
-    local_part = jnp.einsum("asc,as->ca", along_depth, band_pick, precision=EXACT)
-    local_full = lax.dynamic_update_slice(
-        jnp.zeros((3, atom_count), jnp.float32), local_part, (start_zero, band_start)
-    )
-    local_total = lax.psum(local_full, ("band", "ga"))
     bands_here = psi.shape[2]
     waves_here = psi.shape[0]
     psi_flat = psi.reshape(waves_here, 2 * bands_here)
@@ -202,7 +202,7 @@
     nonlocal_full = lax.dynamic_update_slice(
         jnp.zeros((3, atom_count), jnp.float32), nonlocal_part, (start_zero, ga_start)
     )
-    forces = local_total + lax.psum(nonlocal_full, ("band", "ga"))
+    forces = lax.psum(local_part + nonlocal_full, ("band", "ga"))
     return (density_sticks, forces)
 
 

time: 760 us -> 489 us (0.64); the launches traced: 747 us -> 485 us
  local copies, waits for them, and re-layouts: 346 us -> 197 us
  waiting for transfers between devices: 68.2 us -> 12.4 us
  matrix products: 168 us -> 123 us
  other arithmetic: 92.7 us -> 79.5 us
    unnamed x39 -> x19, local copies, waits for them, and re-layouts: 175 us -> 88.5 us
    reduce_scatter x1, waiting for transfers between devices: 68.2 us -> 0.01 us  [shards(): lax.psum_scatter(lax.map(one_block, starts).reshape(share_rows * lax.axis...]
    gather x1, local copies, waits for them, and re-layouts: 73.2 us -> 22.7 us  [shards(): picked_rows = jnp.take(columns.T, share_columns, axis=0)]
    dot_general x14 -> x8, matrix products: 70.3 us -> 25 us  [the longest x1 6.1 us: shards(): jnp.dot(xpass_real, sin_y, precision=FINE)]
    all_to_all x2 -> x0, local copies, waits for them, and re-layouts: 17.3 us -> none  [shards(): lax.all_to_all(chosen, 'ga', split_axis=2, concat_axis=1, tiled=True)]
    reshape x2, local copies, waits for them, and re-layouts: 20.9 us -> 3.75 us  [the longest x1 2.83 us: shards(): picked_rows.T.reshape(2 * planes, ga_count, sub_sticks).transpose(1, 0, 2)]
    all_to_all x1, waiting for transfers between devices: 0.01 us -> 12.4 us  [shards(): lax.all_to_all(chosen, 'ga', split_axis=0, concat_axis=0, tiled=True)]
    all_to_all x1 -> x0, other arithmetic: 10.4 us -> none  [shards(): lax.all_to_all(chosen, 'ga', split_axis=2, concat_axis=1, tiled=True)]
  transfers between devices with their start and end apart: 2 -> 3, of which waited for: 1 -> 1; matrix products, arithmetic and copies ran while one was open for 35% -> 23% of each run, Pallas kernels for 0% -> 0%
where the time goes in v1:
time: 489 us; the launch traced here: 485 us
  local copies, waits for them, and re-layouts  197 us (40%)
  matrix products  123 us (25%)
  other arithmetic  79.5 us (16%)
  blocking collectives  38.7 us (8%)
  between operations  15.8 us (3%)
  waiting for transfers between devices  12.4 us (3%)
  loops' own time  10.7 us (2%)
  starting transfers between devices  7.64 us (2%)
    dot_general x4, matrix products, project_block(): jnp.dot(table.reshape(block_rows * 8, waves_here), psi_flat, preferred_el...  96.8 us
    unnamed x19, local copies, waits for them, and re-layouts  88.5 us
    psum x1, blocking collectives, shards(): forces = lax.psum(local_part + nonlocal_full, ('band', 'ga'))  38.7 us
    another operation x4, other arithmetic, project_block(): jnp.stack([radial * jnp.cos(phase)[:, None, :], radial * jnp.sin(phase)[:...  24.7 us
    gather x1, local copies, waits for them, and re-layouts, shards(): picked_rows = jnp.take(columns.T, share_columns, axis=0)  22.7 us
    cos x4, other arithmetic, project_block(): jnp.cos(phase)[:, None, :]  20.9 us
    all_to_all x1, waiting for transfers between devices, shards(): lax.all_to_all(chosen, 'ga', split_axis=0, concat_axis=0, tiled=True)  12.4 us
    another operation x1, loops' own time, shards(): lax.map(one_block, starts)  10.7 us
  transfers between devices with their start and end apart: 3, of which 1 were waited for; matrix products, arithmetic and copies ran while one was open for 23% of the time, Pallas kernels for 0%

profile of v1, /device:TPU:0, one launch (start us, length us, event | category | flops | bytes accessed | tf_op | source)
XLA Modules:
  0.0 484.9 jit_solution(1100664189729486365)
XLA Ops:
  12.0 83.8 %copy.56 = bf16[33792,2,256]{0,2,1:T(8,128)(2,1)} copy(bf16[33792,2,256]{2,1,0:T(2,128)(2,1)} %param.18) | data formatting | bytes 69206016 | tf_op args[5]
  98.0 206.9 %while.12 = (s32[]{:T(128)}, f32[4,64,2048]{2,1,0:T(8,128)}, s32[4]{0:T(128)}, s32[32]{0:T(128)S(1)}, f32[2,8,33792]{2,1,0:T(8,128)}, /*index=5*/f32[3,32]{1,0:T...) while((s32[]{:T(128)}, f32[4,64,2048]{2,1,0:T(8,128)}, ...), condition=%wide.region_3.4_spmd, body=%wide.region_2.3_spmd.sunk | while | flops 17768366080 | bytes 134012464 | solution.py:178
  103.8 5.2 %fusion.115 = (f32[8,33792]{1,0:T(8,128)}, f32[8,33792]{1,0:T(8,128)}) fusion(f32[33792]{0:T(1024)S(1)} %bitcast.204, f32[8]{0:T(128)S(1)} %get-tuple-element.244, f32[33792]{0:T(1024)S(1)} %bitcast.205, f32[8]{0:T(128)S(1)} %get-tuple-element.246, f32[33792]{0:T(1024)S(1)} %bitcast.203, f32[8]{0:T(128)S(1)} %get-tuple-element.248), kind=kLoop, calls=%fused_computation.14.clone.1 | loop fusion | flops 1622016 | bytes 2568288 | tf_op jit(solution)/shard_map/while/body/eval_jaxpr/cos | solution.py:157
  113.8 6.2 %pad_maximum_fusion.8 = f32[64,2,33792]{2,0,1:T(8,128)} fusion(f32[64,1,33792]{2,0,1:T(8,128)S(1)} %get-tuple-element.255, f32[64,1,33792]{2,0,1:T(8,128)S(1)} %get-tuple-element.256), kind=kLoop, calls=%fused_computation.6.clone.1 | loop fusion | flops 4325376 | bytes 34603008 | tf_op jit(solution)/shard_map/while/body/eval_jaxpr/stack | solution.py:156
  120.0 24.2 %fusion.116 = f32[64,4,2,2,256]{4,0,3,2,1:T(8,128)S(1)} fusion(bf16[2,256,33792,1,1]{2,1,0,4,3:T(8,128)(2,1)} %bitcast.198, f32[4,33792]{1,0:T(4,128)S(1)} %copy-done.5, f32[64,2,33792]{2,0,1:T(8,128)} %pad_maximum_fusion.8), kind=kOutput, calls=%fused_computation.3.clone.1 | convolution fusion | flops 17751343104 | bytes 53493760 | tf_op jit(solution)/shard_map/while/body/eval_jaxpr/dot_general | solution.py:160
  155.5 5.2 %fusion.115 = (f32[8,33792]{1,0:T(8,128)}, f32[8,33792]{1,0:T(8,128)}) fusion(f32[33792]{0:T(1024)S(1)} %bitcast.204, f32[8]{0:T(128)S(1)} %get-tuple-element.244, f32[33792]{0:T(1024)S(1)} %bitcast.205, f32[8]{0:T(128)S(1)} %get-tuple-element.246, f32[33792]{0:T(1024)S(1)} %bitcast.203, f32[8]{0:T(128)S(1)} %get-tuple-element.248), kind=kLoop, calls=%fused_computation.14.clone.1 | loop fusion | flops 1622016 | bytes 2568288 | tf_op jit(solution)/shard_map/while/body/eval_jaxpr/cos | solution.py:157
  165.5 6.2 %pad_maximum_fusion.8 = f32[64,2,33792]{2,0,1:T(8,128)} fusion(f32[64,1,33792]{2,0,1:T(8,128)S(1)} %get-tuple-element.255, f32[64,1,33792]{2,0,1:T(8,128)S(1)} %get-tuple-element.256), kind=kLoop, calls=%fused_computation.6.clone.1 | loop fusion | flops 4325376 | bytes 34603008 | tf_op jit(solution)/shard_map/while/body/eval_jaxpr/stack | solution.py:156
  171.7 24.2 %fusion.116 = f32[64,4,2,2,256]{4,0,3,2,1:T(8,128)S(1)} fusion(bf16[2,256,33792,1,1]{2,1,0,4,3:T(8,128)(2,1)} %bitcast.198, f32[4,33792]{1,0:T(4,128)S(1)} %copy-done.5, f32[64,2,33792]{2,0,1:T(8,128)} %pad_maximum_fusion.8), kind=kOutput, calls=%fused_computation.3.clone.1 | convolution fusion | flops 17751343104 | bytes 53493760 | tf_op jit(solution)/shard_map/while/body/eval_jaxpr/dot_general | solution.py:160
  207.3 5.2 %fusion.115 = (f32[8,33792]{1,0:T(8,128)}, f32[8,33792]{1,0:T(8,128)}) fusion(f32[33792]{0:T(1024)S(1)} %bitcast.204, f32[8]{0:T(128)S(1)} %get-tuple-element.244, f32[33792]{0:T(1024)S(1)} %bitcast.205, f32[8]{0:T(128)S(1)} %get-tuple-element.246, f32[33792]{0:T(1024)S(1)} %bitcast.203, f32[8]{0:T(128)S(1)} %get-tuple-element.248), kind=kLoop, calls=%fused_computation.14.clone.1 | loop fusion | flops 1622016 | bytes 2568288 | tf_op jit(solution)/shard_map/while/body/eval_jaxpr/cos | solution.py:157
  217.3 6.2 %pad_maximum_fusion.8 = f32[64,2,33792]{2,0,1:T(8,128)} fusion(f32[64,1,33792]{2,0,1:T(8,128)S(1)} %get-tuple-element.255, f32[64,1,33792]{2,0,1:T(8,128)S(1)} %get-tuple-element.256), kind=kLoop, calls=%fused_computation.6.clone.1 | loop fusion | flops 4325376 | bytes 34603008 | tf_op jit(solution)/shard_map/while/body/eval_jaxpr/stack | solution.py:156
  223.4 24.2 %fusion.116 = f32[64,4,2,2,256]{4,0,3,2,1:T(8,128)S(1)} fusion(bf16[2,256,33792,1,1]{2,1,0,4,3:T(8,128)(2,1)} %bitcast.198, f32[4,33792]{1,0:T(4,128)S(1)} %copy-done.5, f32[64,2,33792]{2,0,1:T(8,128)} %pad_maximum_fusion.8), kind=kOutput, calls=%fused_computation.3.clone.1 | convolution fusion | flops 17751343104 | bytes 53493760 | tf_op jit(solution)/shard_map/while/body/eval_jaxpr/dot_general | solution.py:160
  259.0 5.2 %fusion.115 = (f32[8,33792]{1,0:T(8,128)}, f32[8,33792]{1,0:T(8,128)}) fusion(f32[33792]{0:T(1024)S(1)} %bitcast.204, f32[8]{0:T(128)S(1)} %get-tuple-element.244, f32[33792]{0:T(1024)S(1)} %bitcast.205, f32[8]{0:T(128)S(1)} %get-tuple-element.246, f32[33792]{0:T(1024)S(1)} %bitcast.203, f32[8]{0:T(128)S(1)} %get-tuple-element.248), kind=kLoop, calls=%fused_computation.14.clone.1 | loop fusion | flops 1622016 | bytes 2568288 | tf_op jit(solution)/shard_map/while/body/eval_jaxpr/cos | solution.py:157
  269.0 6.2 %pad_maximum_fusion.8 = f32[64,2,33792]{2,0,1:T(8,128)} fusion(f32[64,1,33792]{2,0,1:T(8,128)S(1)} %get-tuple-element.255, f32[64,1,33792]{2,0,1:T(8,128)S(1)} %get-tuple-element.256), kind=kLoop, calls=%fused_computation.6.clone.1 | loop fusion | flops 4325376 | bytes 34603008 | tf_op jit(solution)/shard_map/while/body/eval_jaxpr/stack | solution.py:156
  275.2 24.2 %fusion.116 = f32[64,4,2,2,256]{4,0,3,2,1:T(8,128)S(1)} fusion(bf16[2,256,33792,1,1]{2,1,0,4,3:T(8,128)(2,1)} %bitcast.198, f32[4,33792]{1,0:T(4,128)S(1)} %copy-done.5, f32[64,2,33792]{2,0,1:T(8,128)} %pad_maximum_fusion.8), kind=kOutput, calls=%fused_computation.3.clone.1 | convolution fusion | flops 17751343104 | bytes 53493760 | tf_op jit(solution)/shard_map/while/body/eval_jaxpr/dot_general | solution.py:160
  307.8 2.5 fusion.15
  314.1 3.5 fusion.55
  317.7 3.6 convolution_add_fusion
  321.3 3.4 copy.50
  324.7 5.5 %reshape.1345 = f32[20,25600]{1,0:T(8,128)} reshape(f32[3200,160]{1,0:T(8,128)} %copy.50) | data formatting | bytes 4096000 | tf_op jit(solution)/shard_map/reshape | solution.py:69
  330.2 6.1 %convolution_subtract_fusion = f32[3200,160]{0,1:T(8,128)} fusion(f32[3200,160]{0,1:T(8,128)} %fusion.55, f32[3200,160]{1,0:T(8,128)} %bitcast.200), kind=kOutput, calls=%fused_computation.31 | convolution fusion | flops 492262400 | bytes 6144000 | tf_op jit(solution)/shard_map/dot_general | solution.py:65
  336.3 3.5 copy.51
  339.7 5.4 %reshape.1346 = f32[20,25600]{1,0:T(8,128)} reshape(f32[3200,160]{1,0:T(8,128)} %copy.51) | data formatting | bytes 4096000 | tf_op jit(solution)/shard_map/reshape | solution.py:69
  345.2 4.7 pad_maximum_fusion.2
  349.9 9.0 %copy.52 = f32[40,25600]{0,1:T(8,128)} copy(f32[40,25600]{1,0:T(8,128)} %pad_maximum_fusion.2) | data formatting | bytes 8192000 | tf_op jit(solution)/shard_map/concatenate | solution.py:68
  359.0 22.7 %gather_fusion = f32[5120,40]{1,0:T(8,128)} fusion(f32[25600,40]{1,0:T(8,128)} %bitcast.196, s32[5120]{0:T(1024)S(1)} %broadcast_clamp_fusion), kind=kCustom, calls=%fused_computation | custom fusion | bytes 1658880 | tf_op jit(solution)/shard_map/jit(_take)/gather | solution.py:75
  381.7 5.3 %broadcast_select_fusion = f32[5120,40]{1,0:T(8,128)} fusion(f32[5120,40]{1,0:T(8,128)} %gather_fusion, pred[5120]{0:T(1024)(128)(4,1)S(1)} %compare_and_fusion), kind=kLoop, calls=%fused_computation.41 | loop fusion | flops 204800 | bytes 1643520 | tf_op jit(solution)/shard_map/jit(_take)/select_n | solution.py:75
  387.0 2.8 copy.53
  389.8 7.3 %all-to-all-start = ((f32[8,40,640]{2,1,0:T(8,128)}), f32[8,40,640]{2,1,0:T(8,128)}, u32[]{:S(2)}, u32[]{:S(2)}) async-start(f32[8,40,640]{2,1,0:T(8,128)} %bitcast.207), calls=%async_computation | async-start | bytes 1638400 | tf_op jit(solution)/shard_map/all_to_all | solution.py:77
  405.7 12.4 %all-to-all-done = f32[8,40,640]{2,1,0:T(8,128)} async-done(((f32[8,40,640]{2,1,0:T(8,128)}), f32[8,40,640]{2,1,0:T(8,128)}, u32[]{:S(2)}, u32[]{:S(2)}) %all-to-all-start) | async-done | bytes 819232 | tf_op jit(solution)/shard_map/all_to_all | solution.py:77
  418.1 3.0 fusion.27
  434.9 38.7 %psum.7 = f32[3,32]{1,0:T(4,128)} all-reduce(f32[3,32]{1,0:T(4,128)} %add.270), channel_id=1, replica_groups=mesh['band'=4,'ga'=8] {'band','ga'}, use_global_device_ids=true, to_apply=%region_6.7 | all-reduce | flops 96 | bytes 768 | tf_op jit(solution)/shard_map/psum | solution.py:205
  473.6 3.9 copy.109
  (166 shorter events, 88.8 us)
Async XLA Ops:
  8.0 299.8 %copy-start = (f32[20,160,160]{2,1,0:T(8,128)S(1)}, f32[20,160,160]{2,1,0:T(8,128)}, u32[]{:S(2)}) copy-start(f32[20,160,160]{2,1,0:T(8,128)} %param.13) | copy-start | bytes 6144004
  8.0 421.8 %reduce-scatter.2.cloned.1.call-start = ((), (), s32[]{:S(2)}) async-start(), calls=%async_computation.3 | async-start | bytes 2359296 | tf_op jit(solution)/shard_map/reduce_scatter | solution.py:177
  10.1 0.8 copy-start.4
  12.0 86.0 %copy-start.6 = (f32[3,32]{1,0:T(4,128)S(1)}, f32[3,32]{1,0:T(4,128)}, u32[]{:S(2)}) copy-start(f32[3,32]{1,0:T(4,128)} %param.16) | copy-start | bytes 1156
  12.0 86.0 %copy-start.8 = (s32[32]{0:T(128)S(1)}, s32[32]{0:T(128)}, u32[]{:S(2)}) copy-start(s32[32]{0:T(128)} %param.17) | copy-start | bytes 388
  109.4 1.9 copy-start.1
  109.4 2.2 copy-start.2
  113.8 6.2 %copy-start.5 = (f32[4,33792]{1,0:T(4,128)S(1)}, f32[4,33792]{1,0:T(4,128)}, u32[]{:S(2)}) copy-start(f32[4,33792]{1,0:T(4,128)} %get-tuple-element.294) | copy-start | bytes 1622020 | tf_op jit(solution)/shard_map/while
  161.1 1.9 copy-start.1
  161.1 2.2 copy-start.2
  165.5 6.2 %copy-start.5 = (f32[4,33792]{1,0:T(4,128)S(1)}, f32[4,33792]{1,0:T(4,128)}, u32[]{:S(2)}) copy-start(f32[4,33792]{1,0:T(4,128)} %get-tuple-element.294) | copy-start | bytes 1622020 | tf_op jit(solution)/shard_map/while
  212.9 1.9 copy-start.1
  212.9 2.2 copy-start.2
  217.3 6.2 %copy-start.5 = (f32[4,33792]{1,0:T(4,128)S(1)}, f32[4,33792]{1,0:T(4,128)}, u32[]{:S(2)}) copy-start(f32[4,33792]{1,0:T(4,128)} %get-tuple-element.294) | copy-start | bytes 1622020 | tf_op jit(solution)/shard_map/while
  264.6 1.9 copy-start.1
  264.6 2.2 copy-start.2
  269.0 6.2 %copy-start.5 = (f32[4,33792]{1,0:T(4,128)S(1)}, f32[4,33792]{1,0:T(4,128)}, u32[]{:S(2)}) copy-start(f32[4,33792]{1,0:T(4,128)} %get-tuple-element.294) | copy-start | bytes 1622020 | tf_op jit(solution)/shard_map/while
  310.3 3.9 copy-start.3
  389.8 28.3 %all-to-all-start = ((f32[8,40,640]{2,1,0:T(8,128)}), f32[8,40,640]{2,1,0:T(8,128)}, u32[]{:S(2)}, u32[]{:S(2)}) async-start(f32[8,40,640]{2,1,0:T(8,128)} %bitcast.207), calls=%async_computation | async-start | bytes 1638400 | tf_op jit(solution)/shard_map/all_to_all | solution.py:77
  397.1 76.5 %all-gather.2.cloned.1.call-start = ((), (), s32[]{:S(2)}) async-start(), calls=%async_computation.2 | async-start | bytes 4096000 | tf_op jit(solution)/shard_map/all_gather | solution.py:86
  398.3 24.5 %copy-start.10 = (f32[2,8,8]{2,1,0:T(8,128)S(1)}, f32[2,8,8]{2,1,0:T(8,128)}, u32[]{:S(2)}) copy-start(f32[2,8,8]{2,1,0:T(8,128)} %param.22) | copy-start | bytes 1540
  401.0 23.3 %copy-start.9 = (s32[32]{0:T(128)S(1)}, s32[32]{0:T(128)}, u32[]{:S(2)}) copy-start(s32[32]{0:T(128)} %param.17) | copy-start | bytes 388
  401.0 23.3 %copy-start.7 = (f32[3,32]{1,0:T(4,128)S(1)}, f32[3,32]{1,0:T(4,128)}, u32[]{:S(2)}) copy-start(f32[3,32]{1,0:T(4,128)} %param.16) | copy-start | bytes 1156
Sparse Core Ops, SparseCore 0:
  305.0 70.9 reduce-scatter.1
Sparse Core Ops, SparseCore 1:
  421.2 28.7 all-gather.1
